TPU v7x, 32 devices: a whole 2x2x4 slice. The times are simulated.
32 devices in a mesh: rep: 2 (over y), sample: 4 (over z), head: 4 (over x, core).
Axes of the slice: x: 2, y: 2, z: 4, core: 2. Of those that a mesh axis runs over, the one named last changes fastest.
Arguments:
- x_pre: bfloat16 [8, 128, 8192], P(('rep', 'sample'), None, 'head'), parts along dimension 0, may hold values from -120 to 120
- z_pre: bfloat16 [8, 128, 8192], P(('rep', 'sample'), None, 'head'), parts along dimension 0, may hold values from -6 to 6
- b_pre: bfloat16 [8, 128, 512], P(('rep', 'sample')), parts along dimension 0, may hold values from -1.796875 to 1.796875
- c_pre: bfloat16 [8, 128, 512], P(('rep', 'sample')), parts along dimension 0, may hold values from -0.5390625 to 0.5390625
- dt_pre: float32 [8, 128, 128], P(('rep', 'sample'), None, 'head'), parts along dimension 0, may hold values from -1.5 to 7.5
- lengths: int32 [8], P(('rep', 'sample')), parts along dimension 0, may hold values from 64 to 128, as said below
- init_state: float32 [8, 128, 8192], P(('rep', 'sample'), None, 'head'), parts along dimension 0, may hold values from -6 to 6
- a_rates: float32 [128], P('head'), may hold values from 0.005 to 0.3
- dt_bias: float32 [128], P('head'), may hold values from -2 to -1
- skip_scale: float32 [128], P('head'), may hold values from 0.5 to 2
- norm_gain: float32 [8192], P('head'), may hold values from 0.5 to 1.5
- x_dec: bfloat16 [8, 4, 8192], P(('rep', 'sample'), None, 'head'), parts along dimension 0, may hold values from -120 to 120
- z_dec: bfloat16 [8, 4, 8192], P(('rep', 'sample'), None, 'head'), parts along dimension 0, may hold values from -6 to 6
- b_dec: bfloat16 [8, 4, 512], P(('rep', 'sample')), parts along dimension 0, may hold values from -6 to 6
- c_dec: bfloat16 [8, 4, 512], P(('rep', 'sample')), parts along dimension 0, may hold values from -0.5390625 to 0.5390625
- dt_dec: float32 [8, 4, 128], P(('rep', 'sample'), None, 'head'), parts along dimension 0, may hold values from -3 to 3
Outputs:
- out_pre: bfloat16 [8, 128, 8192], P(('rep', 'sample'), None, 'head'), parts along dimension 0
- final_state: bfloat16 [8, 128, 8192], P(('rep', 'sample'), None, 'head'), parts along dimension 0
- out_dec: bfloat16 [8, 4, 8192], P(('rep', 'sample'), None, 'head'), parts along dimension 0
There are 2 independent parts, one for each index of `rep`. A program takes and returns all parts, laid end to end along the dimension named above; an argument that names none is the same for every part. Nothing has to cross between parts.
Inputs may be any that keep to these rules, and one draw needn't show every extreme that they name: Each prompt's valid tokens are the first lengths[p] of its 128 positions; some prompt uses all 128.
All inputs are finite; a program needn't handle non-finite values.
Results may differ from a plain program's by a relative error of at most 0.006.
Values may be sent and summed in bfloat16 or wider, within the bound.
No kernel may reach another device: no remote copies, remote signals or barrier semaphores. Data moves between devices by JAX's collectives and lax.ppermute only.
A program may use at most 64 MiB of HBM per device.

v0:
```python
import jax
import jax.numpy as jnp
from jax import lax
from jax.sharding import PartitionSpec as P

H = 128
P_SIZE = 64
G = 4
BLOCK = 128
epsilon = 1e-05
highest = lax.Precision.HIGHEST


def group_owners(first_head, head_count):
    head_ids = first_head + jnp.arange(head_count, dtype=jnp.int32)
    return head_ids // (H // G)


def group_pick(owners):
    return (owners[:, None] == jnp.arange(G, dtype=jnp.int32)[None, :]).astype(jnp.float32)


def scan_prompt(inputs, b_rows, c_rows, step_delta, rates, skip_gain, start_state, owners):
    length = inputs.shape[0]
    head_count = step_delta.shape[1]
    head_width = inputs.shape[1] // head_count
    states = b_rows.shape[1] // G
    blocks = length // BLOCK
    b_groups = b_rows.reshape(blocks, BLOCK, G, states)
    c_groups = c_rows.reshape(blocks, BLOCK, G, states)
    group_scores = jnp.einsum(
        "cign,cjgn->cijg", c_groups, b_groups, preferred_element_type=jnp.float32
    )
    head_scores = jnp.take(group_scores, owners, axis=3)
    b_head = jnp.take(b_groups, owners, axis=2).astype(jnp.float32)
    c_head = jnp.take(c_groups, owners, axis=2).astype(jnp.float32)
    values = inputs.astype(jnp.float32).reshape(blocks, BLOCK, head_count, head_width)
    block_delta = step_delta.reshape(blocks, BLOCK, head_count)
    decays = jnp.cumsum(-block_delta * rates, axis=1)
    causal_mask = (jnp.arange(BLOCK)[:, None] >= jnp.arange(BLOCK)[None, :])[None, :, :, None]
    spread = decays[:, :, None, :] - decays[:, None, :, :]
    weights = jnp.where(causal_mask, jnp.exp(jnp.where(causal_mask, spread, 0.0)), 0.0)
    scores = head_scores * weights * block_delta[:, None, :, :]
    inner_part = jnp.einsum("cijh,cjhp->cihp", scores, values, precision=highest)
    tail_decay = jnp.exp(decays[:, -1:, :] - decays) * block_delta
    block_states = jnp.einsum(
        "cjhn,cjhp->cnhp", b_head * tail_decay[..., None], values, precision=highest
    )
    block_totals = jnp.exp(decays[:, -1, :])

    def carry_step(carried, pieces):
        factor, fresh_term = pieces
        return (factor[None, :, None] * carried + fresh_term, carried)

    final_carry, starts = lax.scan(
        carry_step,
        start_state.reshape(states, head_count, head_width),
        (block_totals, block_states),
    )
    outer_part = (
        jnp.einsum("cihn,cnhp->cihp", c_head, starts, precision=highest)
        * jnp.exp(decays)[..., None]
    )
    result = inner_part + outer_part + skip_gain[None, None, :, None] * values
    return (
        result.reshape(length, head_count * head_width),
        final_carry.reshape(states, head_count * head_width),
    )


def gate_values(result, gate_rows):
    gate_rows = gate_rows.astype(jnp.float32)
    return result * gate_rows * jax.nn.sigmoid(gate_rows)


def select_heads(c_rows, owners):
    shape_front = c_rows.shape[:2]
    states = c_rows.shape[2] // G
    grouped = c_rows.reshape(shape_front[0], shape_front[1], G, states)
    return jnp.take(grouped, owners, axis=2)


def body(
    x_pre,
    z_pre,
    b_pre,
    c_pre,
    dt_pre,
    lengths,
    init_state,
    a_rates,
    dt_bias,
    skip_scale,
    norm_gain,
    x_dec,
    z_dec,
    b_dec,
    c_dec,
    dt_dec,
):
    heads_here = a_rates.shape[0]
    head_width = x_pre.shape[2] // heads_here
    first_head = lax.axis_index("head") * heads_here
    owners = group_owners(first_head, heads_here)
    picker = group_pick(owners)
    length = x_pre.shape[1]
    positions = jnp.arange(length, dtype=jnp.int32)
    valid_mask = (positions[None, :] < lengths[:, None]).astype(jnp.float32)
    step_delta = jax.nn.softplus(dt_pre + dt_bias) * valid_mask[:, :, None]

    def one_prompt(pieces):
        inputs, b_rows, c_rows, prompt_delta, start_state = pieces
        return scan_prompt(
            inputs, b_rows, c_rows, prompt_delta, a_rates, skip_scale, start_state, owners
        )

    result, final_carry = lax.map(one_prompt, (x_pre, b_pre, c_pre, step_delta, init_state))
    final_state = final_carry.astype(jnp.bfloat16)
    gated_rows = gate_values(result, z_pre)
    pre_totals = lax.psum(jnp.sum(gated_rows * gated_rows, axis=-1), "head")
    norm_scale = lax.rsqrt(pre_totals[:, :, None] / (H * P_SIZE) + epsilon)
    out_pre = (gated_rows * norm_scale * norm_gain * valid_mask[:, :, None]).astype(jnp.bfloat16)
    slots_here = x_dec.shape[0]
    prompt_count = x_dec.shape[1]
    prompts_here = final_state.shape[0]
    states = final_state.shape[1]
    cached = final_state.reshape(prompts_here, states, heads_here, head_width)
    queries = lax.all_to_all(c_dec, "sample", split_axis=1, concat_axis=0, tiled=True)
    c_head = select_heads(queries, owners)
    answers = jnp.einsum("sphn,pnhq->sphq", c_head, cached, preferred_element_type=jnp.float32)
    answers = answers.reshape(answers.shape[0], prompts_here, heads_here * head_width)
    state_reads = lax.all_to_all(
        answers.astype(jnp.bfloat16), "sample", split_axis=0, concat_axis=1, tiled=True
    ).astype(answers.dtype)
    state_reads = state_reads.reshape(slots_here, prompt_count, heads_here, head_width)
    c_groups = c_dec.astype(jnp.float32).reshape(slots_here, prompt_count, G, states)
    b_groups = b_dec.astype(jnp.float32).reshape(slots_here, prompt_count, G, states)
    cb_dot = jnp.einsum("spgn,spgn->spg", c_groups, b_groups, precision=highest)
    cb_dot = jnp.einsum("spg,hg->sph", cb_dot, picker, precision=highest)
    step_sizes = jax.nn.softplus(dt_dec + dt_bias)
    decay_rate = jnp.exp(-step_sizes * a_rates)
    values = x_dec.astype(jnp.float32).reshape(slots_here, prompt_count, heads_here, head_width)
    fresh_term = (
        decay_rate[..., None] * state_reads + (step_sizes * cb_dot + skip_scale)[..., None] * values
    )
    gated_dec = gate_values(
        fresh_term.reshape(slots_here, prompt_count, heads_here * head_width), z_dec
    )
    dec_totals = lax.psum(jnp.sum(gated_dec * gated_dec, axis=-1), "head")
    dec_scale = lax.rsqrt(dec_totals[:, :, None] / (H * P_SIZE) + epsilon)
    out_dec = (gated_dec * dec_scale * norm_gain).astype(jnp.bfloat16)
    return (out_pre, final_state, out_dec)


def solution(mesh):
    in_specs = (
        P(("rep", "sample"), None, "head"),
        P(("rep", "sample"), None, "head"),
        P(("rep", "sample"), None, None),
        P(("rep", "sample"), None, None),
        P(("rep", "sample"), None, "head"),
        P(("rep", "sample")),
        P(("rep", "sample"), None, "head"),
        P("head"),
        P("head"),
        P("head"),
        P("head"),
        P(("rep", "sample"), None, "head"),
        P(("rep", "sample"), None, "head"),
        P(("rep", "sample"), None, None),
        P(("rep", "sample"), None, None),
        P(("rep", "sample"), None, "head"),
    )
    out_specs = (
        P(("rep", "sample"), None, "head"),
        P(("rep", "sample"), None, "head"),
        P(("rep", "sample"), None, "head"),
    )
    return jax.shard_map(body, mesh=mesh, in_specs=in_specs, out_specs=out_specs, check_vma=False)
```

profile of v0, /device:TPU:0, one launch (start us, length us, event | category | flops | bytes accessed | tf_op | source)
XLA Modules:
  0.0 61.4 jit_solution(16359119723385610459)
XLA Ops:
  0.7 0.8 %copy.168 = bf16[1,4,512]{2,0,1:T(2,128)(2,1)S(1)} copy(bf16[1,4,512]{2,1,0:T(4,128)(2,1)} %param.32) | data formatting | bytes 8192 | tf_op args[14]
  1.4 0.5 broadcast.360
  1.9 0.7 %reduce.6 = bf16[4,512]{1,0:T(4,128)(2,1)S(1)} reduce(bf16[4,1,512]{2,1,0:T(2,128)(2,1)S(1)} %bitcast.142, bf16[]{:T(256)} %broadcast.360), dimensions={1}, to_apply=%bitcast.126.reduce_sub_computation | reduce | bytes 8194
  2.6 0.6 reshape.510
  3.2 6.3 %all-to-all-start = ((bf16[4,2,256]{2,1,0:T(2,128)(2,1)}), bf16[4,2,256]{2,1,0:T(2,128)(2,1)}, u32[]{:S(2)}, u32[]{:S(2)}) async-start(bf16[4,2,256]{2,1,0:T(2,128)(2,1)} %reshape.510), calls=%async_computation | async-start | bytes 8192 | tf_op jit(solution)/shard_map/all_to_all | solution.py:128
  10.2 0.8 %negate_multiply_fusion = f32[1,128,32]{1,2,0:T(8,128)S(1)} fusion(f32[32]{0:T(128)} %param.25, f32[128]{0:T(128)S(1)} %compare_convert_fusion, f32[1,128,32]{1,2,0:T(8,128)} %param.22, f32[32]{0:T(128)} %param.26), kind=kLoop, calls=%fused_computation.73 | loop fusion | flops 40960 | bytes 33536 | tf_op jit(solution)/shard_map/while/body/eval_jaxpr/mul | solution.py:39
  11.0 0.1 copy.124
  11.1 0.2 reduce_window_sum.12
  11.3 0.1 copy.138
  11.4 0.6 compare_and_fusion
  11.9 0.6 iota_compare_fusion
  12.6 0.6 compare_select_fusion.3
  13.2 0.9 %reshape.439 = bf16[128,4,128]{2,1,0:T(4,128)(2,1)S(1)} reshape(bf16[1,128,512]{2,1,0:T(8,128)(2,1)} %param.21) | data formatting | bytes 262144 | tf_op jit(solution)/shard_map/reshape.21
  14.1 1.0 %copy.129 = bf16[1,128,512]{1,2,0:T(8,128)(2,1)S(1)} copy(bf16[1,128,512]{2,1,0:T(8,128)(2,1)} %param.21) | data formatting | bytes 262144 | tf_op args[3]
  15.2 2.0 %copy.127 = bf16[1,128,2048]{1,2,0:T(8,128)(2,1)} copy(bf16[1,128,2048]{2,1,0:T(8,128)(2,1)} %param.18) | data formatting | bytes 1048576 | tf_op args[0]
  17.2 1.2 %copy.133 = f32[1,128,2048]{1,2,0:T(8,128)} copy(bf16[1,128,2048]{2,1,0:T(8,128)(2,1)S(1)} %copy-done.2) | data formatting | bytes 1572864 | tf_op jit(solution)/shard_map/while/body/eval_jaxpr/convert_element_type | solution.py:37
  18.4 0.8 %copy.136 = bf16[1,128,512]{1,2,0:T(8,128)(2,1)} copy(bf16[1,128,512]{2,1,0:T(8,128)(2,1)S(1)} %copy-done.6) | data formatting | bytes 262144 | tf_op args[2]
  19.2 0.5 fusion.59
  19.7 0.6 reshape.449
  20.3 0.7 %copy.125 = f32[128,32]{0,1:T(8,128)} copy(f32[128,32]{1,0:T(8,128)S(1)} %bitcast.135) | data formatting | bytes 32768 | tf_op jit(solution)/shard_map/while/body/eval_jaxpr/sub | solution.py:41
  21.0 0.6 pad_clamp_fusion.1
  21.6 0.1 copy.132
  21.7 0.6 pad_clamp_fusion
  22.3 0.1 copy.130
  22.4 0.3 copy.131
  22.8 0.7 %multiply_bitcast_fusion = (f32[128,32]{0,1:T(8,128)}, f32[128,32]{0,1:T(8,128)}) fusion(f32[1,128,32]{1,2,0:T(8,128)S(1)} %copy.138, f32[32]{0:T(128)S(1)} %slice_bitcast_fusion, f32[128]{0:T(128)S(1)} %compare_convert_fusion, f32[1,128,32]{1,2,0:T(8,128)S(1)} %copy-done.8, f32[32]{0:T(128)S(1)} %copy-done.18), kind=kLoop, calls=%fused_computation.72 | loop fusion | flops 40960 | bytes 66304 | tf_op jit(solution)/shard_map/while/body/eval_jaxpr/mul | solution.py:47
  23.5 0.2 convolution_bitcast_fusion.1
  23.7 0.8 %gather_fusion = f32[32,128,128]{1,2,0:T(8,128)S(1)} fusion(f32[128,128,4]{0,1,2:T(8,128)S(1)} %convolution_bitcast_fusion.1, s32[1024]{0:T(1024)} %pad_clamp_fusion.1), kind=kCustom, calls=%fused_computation.2 | custom fusion | bytes 4194432 | tf_op jit(solution)/shard_map/while/body/eval_jaxpr/jit(_take)/gather | solution.py:34
  24.5 1.9 %gather_fusion.2 = bf16[32,128,128]{2,1,0:T(8,128)(2,1)} fusion(bf16[128,4,128]{2,0,1:T(8,128)(2,1)S(1)} %bitcast.129, s32[1024]{0:T(1024)} %pad_clamp_fusion), kind=kCustom, calls=%fused_computation.clone | custom fusion | bytes 2097280 | tf_op jit(solution)/shard_map/while/body/eval_jaxpr/jit(_take)/gather | solution.py:36
  26.5 4.0 %fusion.12 = f32[1,128,32,64]{1,3,2,0:T(8,128)S(1)} fusion(bf16[128,32,64]{0,2,1:T(8,128)(2,1)} %bitcast.137, f32[32,128,128]{1,2,0:T(8,128)S(1)} %gather_fusion, f32[128,32]{0,1:T(8,128)S(1)} %copy-done.17, f32[128,32]{0,1:T(8,128)S(1)} %copy-done.12, pred[32]{0:T(512)(128)(4,1)S(1)} %copy-done.26, pred[128,128]{0,1:T(8,128)(4,1)S(1)} %copy-done.14), kind=kOutput, calls=%fused_computation.16 | convolution fusion | flops 405798912 | bytes 3719200 | tf_op jit(solution)/shard_map/while/body/eval_jaxpr/cijh,cjhp->cihp/dot_general | solution.py:44
  30.5 2.2 %fusion.17 = f32[1,128,32,64]{1,3,2,0:T(8,128)S(1)} fusion(f32[1,128,32,64]{1,3,2,0:T(8,128)S(1)} %fusion.12, f32[128,32,64]{0,2,1:T(8,128)S(1)} %bitcast.131, bf16[32,128,128]{2,1,0:T(8,128)(2,1)S(1)} %copy-done, f32[1,128,32,64]{1,3,2,0:T(8,128)S(1)} %bitcast.132, pred[32]{0:T(512)(128)(4,1)S(1)} %copy-done.26, f32[32]{0:T(128)S(1)} %copy-done.25, ...), kind=kOutput, calls=%fused_computation.20 | convolution fusion | flops 404226048 | bytes 5259424 | tf_op jit(solution)/shard_map/while/body/eval_jaxpr/cihn,cnhp->cihp/dot_general | solution.py:61
  32.7 0.0 copy-start.7
  32.8 0.0 copy-start.19
  32.8 0.0 copy-start.23
  32.8 0.3 copy.134
  33.1 0.0 copy-start.3
  33.2 0.5 copy-done.7
  33.6 0.1 copy.137
  33.8 1.8 %gather_fusion.3 = bf16[32,128,128]{2,1,0:T(8,128)(2,1)} fusion(bf16[128,4,128]{2,0,1:T(8,128)(2,1)S(1)} %bitcast.130, s32[1024]{0:T(1024)} %pad_clamp_fusion), kind=kCustom, calls=%fused_computation.1.clone | custom fusion | bytes 2097280 | tf_op jit(solution)/shard_map/while/body/eval_jaxpr/jit(_take)/gather | solution.py:35
  35.6 0.1 mul.246
  35.6 0.1 mul.247
  35.8 0.4 multiply_reduce_fusion
  36.2 2.7 %fusion = f32[32,128,64]{1,2,0:T(8,128)S(1)} fusion(bf16[128,32,64]{0,2,1:T(8,128)(2,1)S(1)} %bitcast.138, bf16[32,128,128]{2,1,0:T(8,128)(2,1)} %gather_fusion.3, f32[128,32]{0,1:T(8,128)S(1)} %copy-done.16, pred[32]{0:T(512)(128)(4,1)S(1)} %copy-done.27), kind=kOutput, calls=%fused_computation.4 | convolution fusion | flops 404226048 | bytes 2637856 | tf_op jit(solution)/shard_map/while/body/eval_jaxpr/cjhn,cjhp->cnhp/dot_general | solution.py:46
  39.0 0.4 fusion.26
  39.4 0.1 fusion.51
  39.5 0.7 %reshape.511 = bf16[4,1,512]{2,1,0:T(2,128)(2,1)S(1)} reshape(bf16[4,2,256]{2,1,0:T(2,128)(2,1)} %all-to-all-done) | data formatting | bytes 8192
  40.2 0.7 %gather_fusion.1 = bf16[32,4,128]{2,1,0:T(4,128)(2,1)S(1)} fusion(bf16[4,4,128]{2,0,1:T(4,128)(2,1)S(1)} %bitcast.141, s32[1024]{0:T(1024)} %pad_clamp_fusion.1), kind=kCustom, calls=%fused_computation.3 | custom fusion | bytes 65664 | tf_op jit(solution)/shard_map/jit(_take)/gather | solution.py:80
  41.0 0.4 fusion.18
  41.4 0.1 convert_element_type.108
  41.5 0.7 %reduce.7 = bf16[4,2048]{1,0:T(4,128)(2,1)S(1)} reduce(bf16[4,1,2048]{2,1,0:T(2,128)(2,1)S(1)} %convert_element_type.108, bf16[]{:T(256)} %broadcast.360), dimensions={1}, to_apply=%convert_element_type.108.reduce_sub_computation | reduce | bytes 32770 | tf_op jit(solution)/shard_map/convert_element_type | solution.py:133
  42.2 0.6 %reshape.512 = bf16[4,2,1024]{2,1,0:T(2,128)(2,1)} reshape(bf16[4,2048]{1,0:T(4,128)(2,1)S(1)} %reduce.7) | data formatting | bytes 32768
  42.8 5.1 %all-to-all-start.1 = ((bf16[4,2,1024]{2,1,0:T(2,128)(2,1)}), bf16[4,2,1024]{2,1,0:T(2,128)(2,1)S(1)}, u32[]{:S(2)}, u32[]{:S(2)}) async-start(bf16[4,2,1024]{2,1,0:T(2,128)(2,1)} %reshape.512), calls=%async_computation.1 | async-start | bytes 32768 | tf_op jit(solution)/shard_map/all_to_all | solution.py:132
  47.9 0.2 fusion.21
  48.1 1.0 %copy.145 = bf16[1,128,2048]{2,1,0:T(8,128)(2,1)} copy(bf16[1,128,2048]{1,2,0:T(8,128)(2,1)S(1)} %fusion.26) | data formatting | bytes 1048576
  49.2 0.1 mul.262
  49.2 0.1 mul.263
  49.3 0.1 mul.257
  49.4 0.1 mul.258
  49.5 4.0 %all-to-all-done.1 = bf16[4,2,1024]{2,1,0:T(2,128)(2,1)S(1)} async-done(((bf16[4,2,1024]{2,1,0:T(2,128)(2,1)}), bf16[4,2,1024]{2,1,0:T(2,128)(2,1)S(1)}, u32[]{:S(2)}, u32[]{:S(2)}) %all-to-all-start.1) | async-done | bytes 16416 | tf_op jit(solution)/shard_map/all_to_all | solution.py:132
  53.6 0.2 multiply_reduce_fusion.1
  53.8 5.6 %all-reduce = (f32[1,128]{1,0:T(1,128)S(1)}, f32[1,4]{1,0:T(1,128)S(1)}) all-reduce(f32[1,128]{1,0:T(1,128)S(1)} %bitcast.143, f32[1,4]{1,0:T(1,128)S(1)} %bitcast.144), channel_id=1, replica_groups=mesh['rep'=2,'sample'=4,'head'=4] {'head'}, use_global_device_ids=true, to_apply=%region_2.4 | all-reduce | flops 132 | bytes 1056 | tf_op jit(solution)/shard_map/psum | solution.py:120
  59.5 0.1 multiply_convert_fusion.1
  59.6 0.6 %copy.146 = bf16[1,4,2048]{2,1,0:T(4,128)(2,1)} copy(bf16[1,4,2048]{2,0,1:T(2,128)(2,1)S(1)} %multiply_convert_fusion.1) | data formatting | bytes 32768
  60.2 1.2 %multiply_convert_fusion = bf16[1,128,2048]{2,1,0:T(8,128)(2,1)} fusion(f32[128]{0:T(128)S(1)} %copy-done.21, f32[2048]{0:T(1024)S(1)} %copy-done.9, f32[128]{0:T(128)S(1)} %rsqrt_bitcast_fusion.1, f32[1,128,2048]{2,1,0:T(8,128)S(1)} %copy.134, bf16[1,128,2048]{2,1,0:T(8,128)(2,1)S(1)} %copy-done.3), kind=kLoop, calls=%fused_computation.41 | loop fusion | flops 2621440 | bytes 2106368 | tf_op jit(solution)/shard_map/convert_element_type | solution.py:122
  (68 shorter events, 0.3 us)
Async XLA Ops:
  0.6 16.6 %copy-start.2 = (bf16[1,128,2048]{2,1,0:T(8,128)(2,1)S(1)}, bf16[1,128,2048]{2,1,0:T(8,128)(2,1)}, u32[]{:S(2)}) copy-start(bf16[1,128,2048]{2,1,0:T(8,128)(2,1)} %param.18) | copy-start | bytes 1572868
  0.6 17.8 %copy-start.6 = (bf16[1,128,512]{2,1,0:T(8,128)(2,1)S(1)}, bf16[1,128,512]{2,1,0:T(8,128)(2,1)}, u32[]{:S(2)}) copy-start(bf16[1,128,512]{2,1,0:T(8,128)(2,1)} %param.20) | copy-start | bytes 393220
  1.9 17.8 %copy-start.13 = (bf16[1,4,512]{2,1,0:T(4,128)(2,1)S(1)}, bf16[1,4,512]{2,1,0:T(4,128)(2,1)}, u32[]{:S(2)}) copy-start(bf16[1,4,512]{2,1,0:T(4,128)(2,1)} %param.32) | copy-start | bytes 12292
  3.2 36.3 %all-to-all-start = ((bf16[4,2,256]{2,1,0:T(2,128)(2,1)}), bf16[4,2,256]{2,1,0:T(2,128)(2,1)}, u32[]{:S(2)}, u32[]{:S(2)}) async-start(bf16[4,2,256]{2,1,0:T(2,128)(2,1)} %reshape.510), calls=%async_computation | async-start | bytes 8192 | tf_op jit(solution)/shard_map/all_to_all | solution.py:128
  10.2 12.5 %copy-start.20 = (f32[128]{0:T(128)}, f32[128]{0:T(128)S(1)}, u32[]{:S(2)}) copy-start(f32[128]{0:T(128)S(1)} %compare_convert_fusion) | copy-start | bytes 1540
  12.6 9.8 %copy-start.4 = (f32[1,128,2048]{2,1,0:T(8,128)S(1)}, f32[1,128,2048]{2,1,0:T(8,128)}, u32[]{:S(2)}) copy-start(f32[1,128,2048]{2,1,0:T(8,128)} %param.24) | copy-start | bytes 3145732
  17.2 5.6 %copy-start.8 = (f32[1,128,32]{1,2,0:T(8,128)S(1)}, f32[1,128,32]{1,2,0:T(8,128)}, u32[]{:S(2)}) copy-start(f32[1,128,32]{1,2,0:T(8,128)} %param.22) | copy-start | bytes 49156
  17.2 5.6 %copy-start.18 = (f32[32]{0:T(128)S(1)}, f32[32]{0:T(128)}, u32[]{:S(2)}) copy-start(f32[32]{0:T(128)} %param.26) | copy-start | bytes 388
  24.5 2.0 %copy-start.12 = (f32[128,32]{0,1:T(8,128)S(1)}, f32[128,32]{0,1:T(8,128)}, u32[]{:S(2)}) copy-start(f32[128,32]{0,1:T(8,128)} %copy.125) | copy-start | bytes 49156
  24.5 2.0 %copy-start.14 = (pred[128,128]{0,1:T(8,128)(4,1)S(1)}, pred[128,128]{0,1:T(8,128)(4,1)}, u32[]{:S(2)}) copy-start(pred[128,128]{0,1:T(8,128)(4,1)} %iota_compare_fusion) | copy-start | bytes 49156
  24.5 2.0 %copy-start.17 = (f32[128,32]{0,1:T(8,128)S(1)}, f32[128,32]{0,1:T(8,128)}, u32[]{:S(2)}) copy-start(f32[128,32]{0,1:T(8,128)} %get-tuple-element.77) | copy-start | bytes 49156
  24.5 2.0 %copy-start.26 = (pred[32]{0:T(512)(128)(4,1)S(1)}, pred[32]{0:T(512)(128)(4,1)}, u32[]{:S(2)}) copy-start(pred[32]{0:T(512)(128)(4,1)} %compare_and_fusion) | copy-start | bytes 100
  26.5 4.0 %copy-start = (bf16[32,128,128]{2,1,0:T(8,128)(2,1)S(1)}, bf16[32,128,128]{2,1,0:T(8,128)(2,1)}, u32[]{:S(2)}) copy-start(bf16[32,128,128]{2,1,0:T(8,128)(2,1)} %gather_fusion.2) | copy-start | bytes 3145732
  26.5 4.0 %copy-start.1 = (f32[1,128,2048]{1,2,0:T(8,128)S(1)}, f32[1,128,2048]{1,2,0:T(8,128)}, u32[]{:S(2)}) copy-start(f32[1,128,2048]{1,2,0:T(8,128)} %copy.133) | copy-start | bytes 3145732
  26.5 4.0 %copy-start.25 = (f32[32]{0:T(128)S(1)}, f32[32]{0:T(128)}, u32[]{:S(2)}) copy-start(f32[32]{0:T(128)} %param.27) | copy-start | bytes 388
  32.7 0.9 %copy-start.7 = (bf16[1,128,512]{1,2,0:T(8,128)(2,1)S(1)}, bf16[1,128,512]{1,2,0:T(8,128)(2,1)}, u32[]{:S(2)}) copy-start(bf16[1,128,512]{1,2,0:T(8,128)(2,1)} %copy.136) | copy-start | bytes 393220
  32.7 2.8 %copy-start.28 = (f32[32]{0:T(128)S(1)}, f32[32]{0:T(128)}, u32[]{:S(2)}) copy-start(f32[32]{0:T(128)} %fusion.59) | copy-start | bytes 388
  32.8 3.0 %copy-start.22 = (bf16[1,4,512]{2,1,0:T(4,128)(2,1)S(1)}, bf16[1,4,512]{2,1,0:T(4,128)(2,1)}, u32[]{:S(2)}) copy-start(bf16[1,4,512]{2,1,0:T(4,128)(2,1)} %param.31) | copy-start | bytes 12292
  32.8 3.0 %copy-start.19 = (f32[32]{0:T(128)S(1)}, f32[32]{0:T(128)}, u32[]{:S(2)}) copy-start(f32[32]{0:T(128)} %param.26) | copy-start | bytes 388
  32.8 3.0 %copy-start.23 = (f32[32]{0:T(128)S(1)}, f32[32]{0:T(128)}, u32[]{:S(2)}) copy-start(f32[32]{0:T(128)} %param.25) | copy-start | bytes 388
  32.8 2.9 %copy-start.24 = (f32[1,4,32]{2,1,0:T(4,128)S(1)}, f32[1,4,32]{2,1,0:T(4,128)}, u32[]{:S(2)}) copy-start(f32[1,4,32]{2,1,0:T(4,128)} %param.33) | copy-start | bytes 1540
  33.1 2.6 %copy-start.3 = (bf16[1,128,2048]{2,1,0:T(8,128)(2,1)S(1)}, bf16[1,128,2048]{2,1,0:T(8,128)(2,1)}, u32[]{:S(2)}) copy-start(bf16[1,128,2048]{2,1,0:T(8,128)(2,1)} %param.19) | copy-start | bytes 1572868
  33.2 3.0 %copy-start.5 = (bf16[1,128,2048]{1,2,0:T(8,128)(2,1)S(1)}, bf16[1,128,2048]{1,2,0:T(8,128)(2,1)}, u32[]{:S(2)}) copy-start(bf16[1,128,2048]{1,2,0:T(8,128)(2,1)} %copy.127) | copy-start | bytes 1572868
  33.2 3.0 %copy-start.16 = (f32[128,32]{0,1:T(8,128)S(1)}, f32[128,32]{0,1:T(8,128)}, u32[]{:S(2)}) copy-start(f32[128,32]{0,1:T(8,128)} %get-tuple-element.76) | copy-start | bytes 49156
  33.2 3.0 %copy-start.27 = (pred[32]{0:T(512)(128)(4,1)S(1)}, pred[32]{0:T(512)(128)(4,1)}, u32[]{:S(2)}) copy-start(pred[32]{0:T(512)(128)(4,1)} %compare_and_fusion) | copy-start | bytes 100
  36.2 3.2 %copy-start.15 = (bf16[4,4,128]{2,1,0:T(4,128)(2,1)S(1)}, bf16[4,4,128]{2,1,0:T(4,128)(2,1)}, u32[]{:S(2)}) copy-start(bf16[4,4,128]{2,1,0:T(4,128)(2,1)} %reshape.449) | copy-start | bytes 12292
  39.0 9.0 %copy-start.29 = (s32[32]{0:T(128)S(1)}, s32[32]{0:T(128)}, u32[]{:S(2)}) copy-start(s32[32]{0:T(128)} %get-tuple-element.79) | copy-start | bytes 388
  39.0 14.6 %copy-start.10 = (bf16[1,4,2048]{2,1,0:T(4,128)(2,1)S(1)}, bf16[1,4,2048]{2,1,0:T(4,128)(2,1)}, u32[]{:S(2)}) copy-start(bf16[1,4,2048]{2,1,0:T(4,128)(2,1)} %param.30) | copy-start | bytes 49156
  39.0 14.6 %copy-start.11 = (bf16[1,4,2048]{2,1,0:T(4,128)(2,1)S(1)}, bf16[1,4,2048]{2,1,0:T(4,128)(2,1)}, u32[]{:S(2)}) copy-start(bf16[1,4,2048]{2,1,0:T(4,128)(2,1)} %param.29) | copy-start | bytes 49156
  39.0 20.5 %copy-start.9 = (f32[2048]{0:T(1024)S(1)}, f32[2048]{0:T(1024)}, u32[]{:S(2)}) copy-start(f32[2048]{0:T(1024)} %param.28) | copy-start | bytes 24580
  39.0 21.2 %copy-start.21 = (f32[128]{0:T(128)S(1)}, f32[128]{0:T(128)}, u32[]{:S(2)}) copy-start(f32[128]{0:T(128)} %copy-done.20) | copy-start | bytes 1540
  42.8 10.7 %all-to-all-start.1 = ((bf16[4,2,1024]{2,1,0:T(2,128)(2,1)}), bf16[4,2,1024]{2,1,0:T(2,128)(2,1)S(1)}, u32[]{:S(2)}, u32[]{:S(2)}) async-start(bf16[4,2,1024]{2,1,0:T(2,128)(2,1)} %reshape.512), calls=%async_computation.1 | async-start | bytes 32768 | tf_op jit(solution)/shard_map/all_to_all | solution.py:132
where the time goes:
time: 62.1 us; the launch traced here: 61.4 us
  local copies, waits for them, and re-layouts  20.3 us (33%)
  starting transfers between devices  11.4 us (18%)
  matrix products  9.71 us (16%)
  other arithmetic  8.5 us (14%)
  blocking collectives  5.63 us (9%)
  waiting for transfers between devices  4.02 us (6%)
  between operations  1.81 us (3%)
    unnamed x72, local copies, waits for them, and re-layouts  9.6 us
    all_to_all x1, starting transfers between devices, body(): lax.all_to_all(c_dec, 'sample', split_axis=1, concat_axis=0, tiled=True)  6.35 us
    psum x1, blocking collectives, body(): pre_totals = lax.psum(jnp.sum(gated_rows * gated_rows, axis=-1), 'head')  5.63 us
    all_to_all x1, starting transfers between devices, body(): lax.all_to_all(answers.astype(jnp.bfloat16), 'sample', split_axis=0, conc...  5.09 us
    all_to_all x1, waiting for transfers between devices, body(): lax.all_to_all(answers.astype(jnp.bfloat16), 'sample', split_axis=0, conc...  4.01 us
    dot_general x1, matrix products, scan_prompt(): jnp.einsum('cijh,cjhp->cihp', scores, values, precision=highest)  3.96 us
    dot_general x1, matrix products, scan_prompt(): jnp.einsum('cjhn,cjhp->cnhp', b_head * tail_decay[..., None], values, pre...  2.73 us
    dot_general x1, matrix products, scan_prompt(): jnp.einsum('cihn,cnhp->cihp', c_head, starts, precision=highest)  2.2 us
  transfers between devices with their start and end apart: 2, of which 1 were waited for; matrix products, arithmetic and copies ran while one was open for 49% of the time, Pallas kernels for 0%

commit v1 on v0

--- a/solution.py
+++ b/solution.py
@@ -9,6 +9,18 @@
 BLOCK = 128
 epsilon = 1e-05
 highest = lax.Precision.HIGHEST
+
+
+def cut_along(array, dim, count):
+    dims = array.shape
+    tiles = array.reshape(*dims[:dim], count, dims[dim] // count, *dims[dim + 1 :])
+    return jnp.moveaxis(tiles, dim, 0)
+
+
+def laid_out(tiles, dim):
+    tiles = jnp.moveaxis(tiles, 0, dim)
+    shape = tiles.shape
+    return tiles.reshape(*shape[:dim], shape[dim] * shape[dim + 1], *shape[dim + 2 :])
 
 
 def group_owners(first_head, head_count):
@@ -125,7 +137,15 @@
     prompts_here = final_state.shape[0]
     states = final_state.shape[1]
     cached = final_state.reshape(prompts_here, states, heads_here, head_width)
-    queries = lax.all_to_all(c_dec, "sample", split_axis=1, concat_axis=0, tiled=True)
+    size, index = (lax.axis_size("sample"), lax.axis_index("sample"))
+    tiles = cut_along(c_dec, 1, size)
+    out = tiles
+    for step in range(1, size):
+        target, source = ((index + step) % size, (index - step) % size)
+        sent = lax.dynamic_index_in_dim(tiles, target, 0)
+        received = lax.ppermute(sent, "sample", [(i, (i + step) % size) for i in range(size)])
+        out = lax.dynamic_update_slice_in_dim(out, received, source, axis=0)
+    queries = laid_out(out, 0)
     c_head = select_heads(queries, owners)
     answers = jnp.einsum("sphn,pnhq->sphq", c_head, cached, preferred_element_type=jnp.float32)
     answers = answers.reshape(answers.shape[0], prompts_here, heads_here * head_width)

time: 62.1 us -> 61.4 us (0.989)
  local copies, waits for them, and re-layouts: 20.3 us -> 22.1 us
  other arithmetic: 8.5 us -> 7.28 us
  starting transfers between devices: 11.4 us -> 10.2 us
    ppermute x0 -> x3, starting transfers between devices: none -> 6.99 us  [body(): lax.ppermute(sent, 'sample', [(i, (i + step) % size) for i in range(size)])]
    all_to_all x1 -> x0, starting transfers between devices: 6.35 us -> none  [body(): lax.all_to_all(c_dec, 'sample', split_axis=1, concat_axis=0, tiled=True)]
    dynamic_update_slice x0 -> x3, local copies, waits for them, and re-layouts: none -> 2.09 us  [body(): out = lax.dynamic_update_slice_in_dim(out, received, source, axis=0)]
    unnamed x72 -> x61, local copies, waits for them, and re-layouts: 9.6 us -> 7.65 us
    all_to_all x1, starting transfers between devices: 5.09 us -> 3.25 us  [body(): lax.all_to_all(answers.astype(jnp.bfloat16), 'sample', split_axis=0, conc...]
    mul x1, other arithmetic: 0.71 us -> 1.44 us  [scan_prompt(): b_head * tail_decay[..., None]]
    unnamed x1 -> x0, other arithmetic: 0.67 us -> none
    another operation x1, local copies, waits for them, and re-layouts: 0.05 us -> 0.68 us  [scan_prompt(): decays = jnp.cumsum(-block_delta * rates, axis=1)]
  transfers between devices with their start and end apart: 2 -> 4, of which waited for: 1 -> 1; matrix products, arithmetic and copies ran while one was open for 49% -> 52% of each run, Pallas kernels for 0% -> 0%
where the time goes in v1:
time: 61.4 us; the launch traced here: 60.8 us
  local copies, waits for them, and re-layouts  22.1 us (36%)
  starting transfers between devices  10.2 us (17%)
  matrix products  9.7 us (16%)
  other arithmetic  7.28 us (12%)
  blocking collectives  5.63 us (9%)
  waiting for transfers between devices  3.98 us (6%)
  between operations  1.82 us (3%)
    unnamed x61, local copies, waits for them, and re-layouts  7.65 us
    ppermute x3, starting transfers between devices, body(): lax.ppermute(sent, 'sample', [(i, (i + step) % size) for i in range(size)])  6.99 us
    psum x1, blocking collectives, body(): pre_totals = lax.psum(jnp.sum(gated_rows * gated_rows, axis=-1), 'head')  5.63 us
    all_to_all x1, waiting for transfers between devices, body(): lax.all_to_all(answers.astype(jnp.bfloat16), 'sample', split_axis=0, conc...  3.97 us
    dot_general x1, matrix products, scan_prompt(): jnp.einsum('cijh,cjhp->cihp', scores, values, precision=highest)  3.96 us
    all_to_all x1, starting transfers between devices, body(): lax.all_to_all(answers.astype(jnp.bfloat16), 'sample', split_axis=0, conc...  3.25 us
    dot_general x1, matrix products, scan_prompt(): jnp.einsum('cjhn,cjhp->cnhp', b_head * tail_decay[..., None], values, pre...  2.73 us
    dot_general x1, matrix products, scan_prompt(): jnp.einsum('cihn,cnhp->cihp', c_head, starts, precision=highest)  2.2 us
  transfers between devices with their start and end apart: 4, of which 1 were waited for; matrix products, arithmetic and copies ran while one was open for 52% of the time, Pallas kernels for 0%

profile of v1, /device:TPU:0, one launch (start us, length us, event | category | flops | bytes accessed | tf_op | source)
XLA Modules:
  0.0 60.8 jit_solution(10176095810510432195)
XLA Ops:
  0.6 0.0 copy-start.2
  0.7 0.8 %copy.143 = bf16[1,4,512]{2,1,0:T(4,128)(2,1)S(1)} copy(bf16[1,4,512]{2,1,0:T(4,128)(2,1)} %param.32) | data formatting | bytes 8192
  1.4 0.6 dynamic-slice_bitcast_fusion
  2.0 3.1 %collective-permute-start = (bf16[1,1,1,512]{3,0,2,1:T(2,128)(2,1)}, bf16[1,1,1,512]{3,0,2,1:T(2,128)(2,1)}, u32[]{:S(2)}, u32[]{:S(2)}) collective-permute-start(bf16[1,1,1,512]{3,0,2,1:T(2,128)(2,1)} %get-tuple-element.77), channel_id=1, source_target_pairs={{0,4},{4,8},{8,12},{12,0},{1,5},{5,9},{9,13},{13,1},{2,6},{6,10},{... | collective-permute-start | bytes 3080 | tf_op jit(solution)/shard_map/ppermute | solution.py:146
  5.0 2.6 %collective-permute-start.1 = (bf16[1,1,1,512]{3,0,2,1:T(2,128)(2,1)}, bf16[1,1,1,512]{3,0,2,1:T(2,128)(2,1)}, u32[]{:S(2)}, u32[]{:S(2)}) collective-permute-start(bf16[1,1,1,512]{3,0,2,1:T(2,128)(2,1)} %get-tuple-element.76), channel_id=1, source_target_pairs={{0,8},{4,12},{8,0},{12,4},{1,9},{5,13},{9,1},{13,5},{2,10},{6,14},... | collective-permute-start | bytes 3080 | tf_op jit(solution)/shard_map/ppermute | solution.py:146
  7.6 1.3 %collective-permute-start.2 = (bf16[1,1,1,512]{3,0,2,1:T(2,128)(2,1)}, bf16[1,1,1,512]{3,0,2,1:T(2,128)(2,1)}, u32[]{:S(2)}, u32[]{:S(2)}) collective-permute-start(bf16[1,1,1,512]{3,0,2,1:T(2,128)(2,1)} %get-tuple-element.75), channel_id=1, source_target_pairs={{0,12},{4,0},{8,4},{12,8},{1,13},{5,1},{9,5},{13,9},{2,14},{6,2},{... | collective-permute-start | bytes 3080 | tf_op jit(solution)/shard_map/ppermute | solution.py:146
  9.7 0.8 %negate_multiply_fusion = f32[1,128,32]{1,2,0:T(8,128)S(1)} fusion(f32[32]{0:T(128)} %param.25, f32[128]{0:T(128)S(1)} %compare_convert_fusion, f32[1,128,32]{1,2,0:T(8,128)} %param.22, f32[32]{0:T(128)} %param.26), kind=kLoop, calls=%fused_computation.73 | loop fusion | flops 40960 | bytes 33536 | tf_op jit(solution)/shard_map/while/body/eval_jaxpr/mul | solution.py:51
  10.5 0.1 copy.97
  10.6 0.2 reduce_window_sum.12
  10.8 0.7 %copy.111 = f32[1,128,32]{1,2,0:T(8,128)} copy(f32[1,128,32]{2,1,0:T(8,128)S(1)} %reduce_window_sum.12) | data formatting | bytes 32768 | tf_op jit(solution)/shard_map/while/body/eval_jaxpr/jit(cumsum)/reduce_window_sum | solution.py:51
  11.4 0.5 slice_bitcast_fusion
  12.0 0.5 compare_and_fusion
  12.5 0.6 %iota_compare_fusion = pred[128,128]{0,1:T(8,128)(4,1)} fusion(), kind=kLoop, calls=%fused_computation.55 | loop fusion | flops 16384 | bytes 16384 | tf_op jit(solution)/shard_map/while/body/eval_jaxpr/ge | solution.py:52
  13.1 0.9 %reshape.435 = bf16[128,4,128]{2,1,0:T(4,128)(2,1)S(1)} reshape(bf16[1,128,512]{2,1,0:T(8,128)(2,1)} %param.21) | data formatting | bytes 262144 | tf_op jit(solution)/shard_map/reshape.21
  14.1 1.0 %copy.102 = bf16[1,128,512]{1,2,0:T(8,128)(2,1)S(1)} copy(bf16[1,128,512]{2,1,0:T(8,128)(2,1)} %param.21) | data formatting | bytes 262144 | tf_op args[3]
  15.1 0.5 compare_select_fusion.3
  15.6 2.0 %copy.100 = bf16[1,128,2048]{1,2,0:T(8,128)(2,1)} copy(bf16[1,128,2048]{2,1,0:T(8,128)(2,1)} %param.18) | data formatting | bytes 1048576 | tf_op args[0]
  17.7 1.2 %copy.106 = f32[1,128,2048]{1,2,0:T(8,128)} copy(bf16[1,128,2048]{2,1,0:T(8,128)(2,1)S(1)} %copy-done.2) | data formatting | bytes 1572864 | tf_op jit(solution)/shard_map/while/body/eval_jaxpr/convert_element_type | solution.py:49
  18.9 0.6 fusion.59
  19.5 0.8 %copy.109 = bf16[1,128,512]{1,2,0:T(8,128)(2,1)} copy(bf16[1,128,512]{2,1,0:T(8,128)(2,1)S(1)} %copy-done.6) | data formatting | bytes 262144 | tf_op args[2]
  20.3 0.7 %copy.98 = f32[128,32]{0,1:T(8,128)} copy(f32[128,32]{1,0:T(8,128)S(1)} %bitcast.137) | data formatting | bytes 32768 | tf_op jit(solution)/shard_map/while/body/eval_jaxpr/sub | solution.py:53
  21.0 0.3 copy.104
  21.3 0.1 copy.103
  21.5 0.7 %copy.105 = f32[128,32]{0,1:T(8,128)} copy(f32[128,32]{1,0:T(8,128)S(1)} %bitcast_exponential_fusion) | data formatting | bytes 32768 | tf_op jit(solution)/shard_map/while/body/eval_jaxpr/exp | solution.py:74
  22.1 0.2 convolution_bitcast_fusion.1
  22.3 0.7 %gather_fusion = f32[32,128,128]{1,2,0:T(8,128)S(1)} fusion(f32[128,128,4]{0,1,2:T(8,128)S(1)} %convolution_bitcast_fusion.1, s32[1024]{0:T(1024)S(1)} %pad_clamp_fusion.1), kind=kCustom, calls=%fused_computation.2 | custom fusion | bytes 4194432 | tf_op jit(solution)/shard_map/while/body/eval_jaxpr/jit(_take)/gather | solution.py:46
  23.1 1.4 %multiply_bitcast_fusion = (f32[128,32]{0,1:T(8,128)}, f32[128,32]{0,1:T(8,128)S(1)}) fusion(f32[1,128,32]{1,2,0:T(8,128)} %copy.111, f32[32]{0:T(128)} %slice_bitcast_fusion, f32[128]{0:T(128)} %copy-done.16, f32[1,128,32]{1,2,0:T(8,128)} %param.22, f32[32]{0:T(128)} %param.26), kind=kLoop, calls=%fused_computation.72 | loop fusion | flops 40960 | bytes 66304 | tf_op jit(solution)/shard_map/while/body/eval_jaxpr/mul | solution.py:59
  24.5 1.7 %gather_fusion.2 = bf16[32,128,128]{2,1,0:T(8,128)(2,1)} fusion(bf16[128,4,128]{2,0,1:T(8,128)(2,1)S(1)} %bitcast.131, s32[1024]{0:T(1024)S(1)} %pad_clamp_fusion), kind=kCustom, calls=%fused_computation.clone | custom fusion | bytes 2097280 | tf_op jit(solution)/shard_map/while/body/eval_jaxpr/jit(_take)/gather | solution.py:48
  26.2 0.0 copy-start.21
  26.2 4.0 %fusion.12 = f32[1,128,32,64]{1,3,2,0:T(8,128)S(1)} fusion(bf16[128,32,64]{0,2,1:T(8,128)(2,1)} %bitcast.141, f32[32,128,128]{1,2,0:T(8,128)S(1)} %gather_fusion, f32[128,32]{0,1:T(8,128)S(1)} %get-tuple-element.74, f32[128,32]{0,1:T(8,128)S(1)} %copy-done.12, pred[32]{0:T(512)(128)(4,1)S(1)} %copy-done.22, pred[128,128]{0,1:T(8,128)(4,1)S(1)} %copy-done.13), kind=kOutput, calls=%fused_computation.16 | convolution fusion | flops 405798912 | bytes 3719200 | tf_op jit(solution)/shard_map/while/body/eval_jaxpr/cijh,cjhp->cihp/dot_general | solution.py:56
  30.2 2.2 %fusion.17 = f32[1,128,32,64]{1,3,2,0:T(8,128)S(1)} fusion(f32[1,128,32,64]{1,3,2,0:T(8,128)S(1)} %fusion.12, f32[128,32,64]{0,2,1:T(8,128)S(1)} %bitcast.133, bf16[32,128,128]{2,1,0:T(8,128)(2,1)S(1)} %copy-done, f32[1,128,32,64]{1,3,2,0:T(8,128)S(1)} %bitcast.134, pred[32]{0:T(512)(128)(4,1)S(1)} %copy-done.22, f32[32]{0:T(128)S(1)} %copy-done.21, ...), kind=kOutput, calls=%fused_computation.20 | convolution fusion | flops 404226048 | bytes 5259424 | tf_op jit(solution)/shard_map/while/body/eval_jaxpr/cihn,cnhp->cihp/dot_general | solution.py:73
  32.5 0.3 copy.107
  32.9 0.3 copy-done.18
  33.2 0.1 mul.246
  33.3 0.1 mul.247
  33.4 0.1 copy-done.7
  33.4 0.1 copy.110
  33.6 1.7 %gather_fusion.3 = bf16[32,128,128]{2,1,0:T(8,128)(2,1)} fusion(bf16[128,4,128]{2,0,1:T(8,128)(2,1)S(1)} %bitcast.132, s32[1024]{0:T(1024)S(1)} %pad_clamp_fusion), kind=kCustom, calls=%fused_computation.1.clone | custom fusion | bytes 2097280 | tf_op jit(solution)/shard_map/while/body/eval_jaxpr/jit(_take)/gather | solution.py:47
  35.2 0.4 multiply_reduce_fusion
  35.6 0.1 fusion.51
  35.7 2.7 %fusion = f32[32,128,64]{1,2,0:T(8,128)S(1)} fusion(bf16[128,32,64]{0,2,1:T(8,128)(2,1)S(1)} %bitcast.142, bf16[32,128,128]{2,1,0:T(8,128)(2,1)} %gather_fusion.3, f32[128,32]{0,1:T(8,128)S(1)} %copy-done.14, pred[32]{0:T(512)(128)(4,1)S(1)} %copy-done.23), kind=kOutput, calls=%fused_computation.4 | convolution fusion | flops 404226048 | bytes 2637856 | tf_op jit(solution)/shard_map/while/body/eval_jaxpr/cjhn,cjhp->cnhp/dot_general | solution.py:58
  38.5 0.4 fusion.26
  39.0 0.7 %dynamic_update_slice.18 = bf16[4,1,1,512]{3,0,2,1:T(4,128)(2,1)S(1)} dynamic-update-slice(bf16[4,1,1,512]{3,0,2,1:T(4,128)(2,1)S(1)} %bitcast.139, bf16[1,1,1,512]{3,0,2,1:T(2,128)(2,1)} %collective-permute-done, s32[]{:T(128)S(6)} %select_n.147, s32[]{:T(128)} %constant.154.clone.1, s32[]{:T(128)} %constant.154.clone.1, s32[]{:T(128)} %constant.154.clone.1) | dynamic-update-slice | bytes 2052 | tf_op jit(solution)/shard_map/dynamic_update_slice | solution.py:147
  39.6 0.7 %dynamic_update_slice.19 = bf16[4,1,1,512]{3,0,2,1:T(4,128)(2,1)S(1)} dynamic-update-slice(bf16[4,1,1,512]{3,0,2,1:T(4,128)(2,1)S(1)} %dynamic_update_slice.18, bf16[1,1,1,512]{3,0,2,1:T(2,128)(2,1)} %collective-permute-done.1, s32[]{:T(128)S(6)} %select_n.151, s32[]{:T(128)} %constant.154.clone.1, s32[]{:T(128)} %constant.154.clone.1, s32[]{:T(128)} %constant.154.clone.1) | dynamic-update-slice | bytes 2052 | tf_op jit(solution)/shard_map/dynamic_update_slice | solution.py:147
  40.3 0.7 %dynamic_update_slice.20 = bf16[4,1,1,512]{3,0,2,1:T(4,128)(2,1)S(1)} dynamic-update-slice(bf16[4,1,1,512]{3,0,2,1:T(4,128)(2,1)S(1)} %dynamic_update_slice.19, bf16[1,1,1,512]{3,0,2,1:T(2,128)(2,1)} %collective-permute-done.2, s32[]{:T(128)S(6)} %select_n.155, s32[]{:T(128)} %constant.154.clone.1, s32[]{:T(128)} %constant.154.clone.1, s32[]{:T(128)} %constant.154.clone.1) | dynamic-update-slice | bytes 2052 | tf_op jit(solution)/shard_map/dynamic_update_slice | solution.py:147
  41.1 0.6 gather_fusion.1
  41.7 0.4 fusion.18
  42.1 0.1 convert_element_type.108
  42.2 0.5 broadcast.377
  42.7 0.7 %reduce.4 = bf16[4,2048]{1,0:T(4,128)(2,1)S(1)} reduce(bf16[4,1,2048]{2,1,0:T(2,128)(2,1)S(1)} %convert_element_type.108, bf16[]{:T(256)} %broadcast.377), dimensions={1}, to_apply=%convert_element_type.108.reduce_sub_computation | reduce | bytes 32770 | tf_op jit(solution)/shard_map/convert_element_type | solution.py:153
  43.5 0.6 %reshape.504 = bf16[4,2,1024]{2,1,0:T(2,128)(2,1)} reshape(bf16[4,2048]{1,0:T(4,128)(2,1)S(1)} %reduce.4) | data formatting | bytes 32768
  44.1 3.3 %all-to-all-start = ((bf16[4,2,1024]{2,1,0:T(2,128)(2,1)}), bf16[4,2,1024]{2,1,0:T(2,128)(2,1)S(1)}, u32[]{:S(2)}, u32[]{:S(2)}) async-start(bf16[4,2,1024]{2,1,0:T(2,128)(2,1)} %reshape.504), calls=%async_computation | async-start | bytes 32768 | tf_op jit(solution)/shard_map/all_to_all | solution.py:152
  47.4 0.2 fusion.21
  47.5 1.0 %copy.116 = bf16[1,128,2048]{2,1,0:T(8,128)(2,1)} copy(bf16[1,128,2048]{1,2,0:T(8,128)(2,1)S(1)} %fusion.26) | data formatting | bytes 1048576
  48.6 0.1 mul.262
  48.6 0.1 mul.263
  48.8 0.1 mul.257
  48.8 0.1 mul.258
  49.0 4.0 %all-to-all-done = bf16[4,2,1024]{2,1,0:T(2,128)(2,1)S(1)} async-done(((bf16[4,2,1024]{2,1,0:T(2,128)(2,1)}), bf16[4,2,1024]{2,1,0:T(2,128)(2,1)S(1)}, u32[]{:S(2)}, u32[]{:S(2)}) %all-to-all-start) | async-done | bytes 16416 | tf_op jit(solution)/shard_map/all_to_all | solution.py:152
  53.0 0.2 multiply_reduce_fusion.1
  53.2 5.6 %all-reduce = (f32[1,128]{1,0:T(1,128)S(1)}, f32[1,4]{1,0:T(1,128)S(1)}) all-reduce(f32[1,128]{1,0:T(1,128)S(1)} %bitcast.145, f32[1,4]{1,0:T(1,128)S(1)} %bitcast.146), channel_id=1, replica_groups=mesh['rep'=2,'sample'=4,'head'=4] {'head'}, use_global_device_ids=true, to_apply=%region_2.4 | all-reduce | flops 132 | bytes 1056 | tf_op jit(solution)/shard_map/psum | solution.py:132
  58.9 1.2 %multiply_convert_fusion = bf16[1,128,2048]{2,1,0:T(8,128)(2,1)} fusion(f32[128]{0:T(128)S(1)} %copy-done.17, f32[2048]{0:T(1024)S(1)} %copy-done.9, f32[128]{0:T(128)S(1)} %rsqrt_bitcast_fusion.1, f32[1,128,2048]{2,1,0:T(8,128)S(1)} %copy.107, bf16[1,128,2048]{2,1,0:T(8,128)(2,1)S(1)} %copy-done.3), kind=kLoop, calls=%fused_computation.41 | loop fusion | flops 2621440 | bytes 2106368 | tf_op jit(solution)/shard_map/convert_element_type | solution.py:134
  60.1 0.1 multiply_convert_fusion.1
  60.2 0.6 %copy.117 = bf16[1,4,2048]{2,1,0:T(4,128)(2,1)} copy(bf16[1,4,2048]{2,0,1:T(2,128)(2,1)S(1)} %multiply_convert_fusion.1) | data formatting | bytes 32768
  (64 shorter events, 0.3 us)
Async XLA Ops:
  0.6 17.0 %copy-start.2 = (bf16[1,128,2048]{2,1,0:T(8,128)(2,1)S(1)}, bf16[1,128,2048]{2,1,0:T(8,128)(2,1)}, u32[]{:S(2)}) copy-start(bf16[1,128,2048]{2,1,0:T(8,128)(2,1)} %param.18) | copy-start | bytes 1572868
  0.6 18.8 %copy-start.6 = (bf16[1,128,512]{2,1,0:T(8,128)(2,1)S(1)}, bf16[1,128,512]{2,1,0:T(8,128)(2,1)}, u32[]{:S(2)}) copy-start(bf16[1,128,512]{2,1,0:T(8,128)(2,1)} %param.20) | copy-start | bytes 393220
  2.0 36.9 %collective-permute-start = (bf16[1,1,1,512]{3,0,2,1:T(2,128)(2,1)}, bf16[1,1,1,512]{3,0,2,1:T(2,128)(2,1)}, u32[]{:S(2)}, u32[]{:S(2)}) collective-permute-start(bf16[1,1,1,512]{3,0,2,1:T(2,128)(2,1)} %get-tuple-element.77), channel_id=1, source_target_pairs={{0,4},{4,8},{8,12},{12,0},{1,5},{5,9},{9,13},{13,1},{2,6},{6,10},{... | collective-permute-start | bytes 3080 | tf_op jit(solution)/shard_map/ppermute | solution.py:146
  5.0 34.6 %collective-permute-start.1 = (bf16[1,1,1,512]{3,0,2,1:T(2,128)(2,1)}, bf16[1,1,1,512]{3,0,2,1:T(2,128)(2,1)}, u32[]{:S(2)}, u32[]{:S(2)}) collective-permute-start(bf16[1,1,1,512]{3,0,2,1:T(2,128)(2,1)} %get-tuple-element.76), channel_id=1, source_target_pairs={{0,8},{4,12},{8,0},{12,4},{1,9},{5,13},{9,1},{13,5},{2,10},{6,14},... | collective-permute-start | bytes 3080 | tf_op jit(solution)/shard_map/ppermute | solution.py:146
  7.6 32.7 %collective-permute-start.2 = (bf16[1,1,1,512]{3,0,2,1:T(2,128)(2,1)}, bf16[1,1,1,512]{3,0,2,1:T(2,128)(2,1)}, u32[]{:S(2)}, u32[]{:S(2)}) collective-permute-start(bf16[1,1,1,512]{3,0,2,1:T(2,128)(2,1)} %get-tuple-element.75), channel_id=1, source_target_pairs={{0,12},{4,0},{8,4},{12,8},{1,13},{5,1},{9,5},{13,9},{2,14},{6,2},{... | collective-permute-start | bytes 3080 | tf_op jit(solution)/shard_map/ppermute | solution.py:146
  9.6 0.8 %copy-start.16 = (f32[128]{0:T(128)}, f32[128]{0:T(128)S(1)}, u32[]{:S(2)}) copy-start(f32[128]{0:T(128)S(1)} %compare_convert_fusion) | copy-start | bytes 1540
  10.6 10.4 %copy-start.4 = (f32[1,128,2048]{2,1,0:T(8,128)S(1)}, f32[1,128,2048]{2,1,0:T(8,128)}, u32[]{:S(2)}) copy-start(f32[1,128,2048]{2,1,0:T(8,128)} %param.24) | copy-start | bytes 3145732
  23.0 3.2 %copy-start.12 = (f32[128,32]{0,1:T(8,128)S(1)}, f32[128,32]{0,1:T(8,128)}, u32[]{:S(2)}) copy-start(f32[128,32]{0,1:T(8,128)} %copy.98) | copy-start | bytes 49156
  23.0 3.1 %copy-start.13 = (pred[128,128]{0,1:T(8,128)(4,1)S(1)}, pred[128,128]{0,1:T(8,128)(4,1)}, u32[]{:S(2)}) copy-start(pred[128,128]{0,1:T(8,128)(4,1)} %iota_compare_fusion) | copy-start | bytes 49156
  23.0 3.1 %copy-start.22 = (pred[32]{0:T(512)(128)(4,1)S(1)}, pred[32]{0:T(512)(128)(4,1)}, u32[]{:S(2)}) copy-start(pred[32]{0:T(512)(128)(4,1)} %compare_and_fusion) | copy-start | bytes 100
  26.2 4.0 %copy-start = (bf16[32,128,128]{2,1,0:T(8,128)(2,1)S(1)}, bf16[32,128,128]{2,1,0:T(8,128)(2,1)}, u32[]{:S(2)}) copy-start(bf16[32,128,128]{2,1,0:T(8,128)(2,1)} %gather_fusion.2) | copy-start | bytes 3145732
  26.2 4.0 %copy-start.1 = (f32[1,128,2048]{1,2,0:T(8,128)S(1)}, f32[1,128,2048]{1,2,0:T(8,128)}, u32[]{:S(2)}) copy-start(f32[1,128,2048]{1,2,0:T(8,128)} %copy.106) | copy-start | bytes 3145732
  26.2 4.0 %copy-start.8 = (f32[128,32]{0,1:T(8,128)S(1)}, f32[128,32]{0,1:T(8,128)}, u32[]{:S(2)}) copy-start(f32[128,32]{0,1:T(8,128)} %copy.105) | copy-start | bytes 49156
  26.2 4.0 %copy-start.21 = (f32[32]{0:T(128)S(1)}, f32[32]{0:T(128)}, u32[]{:S(2)}) copy-start(f32[32]{0:T(128)} %param.27) | copy-start | bytes 388
  32.4 0.7 %copy-start.18 = (bf16[1,4,512]{2,1,0:T(4,128)(2,1)S(1)}, bf16[1,4,512]{2,1,0:T(4,128)(2,1)}, u32[]{:S(2)}) copy-start(bf16[1,4,512]{2,1,0:T(4,128)(2,1)} %param.31) | copy-start | bytes 12292
  32.5 0.7 %copy-start.15 = (f32[32]{0:T(128)S(1)}, f32[32]{0:T(128)}, u32[]{:S(2)}) copy-start(f32[32]{0:T(128)} %param.26) | copy-start | bytes 388
  32.5 0.7 %copy-start.19 = (f32[32]{0:T(128)S(1)}, f32[32]{0:T(128)}, u32[]{:S(2)}) copy-start(f32[32]{0:T(128)} %param.25) | copy-start | bytes 388
  32.5 0.7 %copy-start.20 = (f32[1,4,32]{2,1,0:T(4,128)S(1)}, f32[1,4,32]{2,1,0:T(4,128)}, u32[]{:S(2)}) copy-start(f32[1,4,32]{2,1,0:T(4,128)} %param.33) | copy-start | bytes 1540
  32.5 0.7 %copy-start.24 = (f32[32]{0:T(128)S(1)}, f32[32]{0:T(128)}, u32[]{:S(2)}) copy-start(f32[32]{0:T(128)} %fusion.59) | copy-start | bytes 388
  32.5 0.9 %copy-start.7 = (bf16[1,128,512]{1,2,0:T(8,128)(2,1)S(1)}, bf16[1,128,512]{1,2,0:T(8,128)(2,1)}, u32[]{:S(2)}) copy-start(bf16[1,128,512]{1,2,0:T(8,128)(2,1)} %copy.109) | copy-start | bytes 393220
  33.1 2.1 %copy-start.3 = (bf16[1,128,2048]{2,1,0:T(8,128)(2,1)S(1)}, bf16[1,128,2048]{2,1,0:T(8,128)(2,1)}, u32[]{:S(2)}) copy-start(bf16[1,128,2048]{2,1,0:T(8,128)(2,1)} %param.19) | copy-start | bytes 1572868
  33.1 2.6 %copy-start.5 = (bf16[1,128,2048]{1,2,0:T(8,128)(2,1)S(1)}, bf16[1,128,2048]{1,2,0:T(8,128)(2,1)}, u32[]{:S(2)}) copy-start(bf16[1,128,2048]{1,2,0:T(8,128)(2,1)} %copy.100) | copy-start | bytes 1572868
  33.1 2.6 %copy-start.14 = (f32[128,32]{0,1:T(8,128)S(1)}, f32[128,32]{0,1:T(8,128)}, u32[]{:S(2)}) copy-start(f32[128,32]{0,1:T(8,128)} %get-tuple-element.73) | copy-start | bytes 49156
  33.1 2.6 %copy-start.23 = (pred[32]{0:T(512)(128)(4,1)S(1)}, pred[32]{0:T(512)(128)(4,1)}, u32[]{:S(2)}) copy-start(pred[32]{0:T(512)(128)(4,1)} %compare_and_fusion) | copy-start | bytes 100
  38.5 8.9 %copy-start.25 = (s32[32]{0:T(128)S(1)}, s32[32]{0:T(128)}, u32[]{:S(2)}) copy-start(s32[32]{0:T(128)} %get-tuple-element.79) | copy-start | bytes 388
  38.5 14.5 %copy-start.10 = (bf16[1,4,2048]{2,1,0:T(4,128)(2,1)S(1)}, bf16[1,4,2048]{2,1,0:T(4,128)(2,1)}, u32[]{:S(2)}) copy-start(bf16[1,4,2048]{2,1,0:T(4,128)(2,1)} %param.30) | copy-start | bytes 49156
  38.5 14.5 %copy-start.11 = (bf16[1,4,2048]{2,1,0:T(4,128)(2,1)S(1)}, bf16[1,4,2048]{2,1,0:T(4,128)(2,1)}, u32[]{:S(2)}) copy-start(bf16[1,4,2048]{2,1,0:T(4,128)(2,1)} %param.29) | copy-start | bytes 49156
  38.5 20.3 %copy-start.9 = (f32[2048]{0:T(1024)S(1)}, f32[2048]{0:T(1024)}, u32[]{:S(2)}) copy-start(f32[2048]{0:T(1024)} %param.28) | copy-start | bytes 24580
  38.5 20.3 %copy-start.17 = (f32[128]{0:T(128)S(1)}, f32[128]{0:T(128)}, u32[]{:S(2)}) copy-start(f32[128]{0:T(128)} %copy-done.16) | copy-start | bytes 1540
  44.1 8.8 %all-to-all-start = ((bf16[4,2,1024]{2,1,0:T(2,128)(2,1)}), bf16[4,2,1024]{2,1,0:T(2,128)(2,1)S(1)}, u32[]{:S(2)}, u32[]{:S(2)}) async-start(bf16[4,2,1024]{2,1,0:T(2,128)(2,1)} %reshape.504), calls=%async_computation | async-start | bytes 32768 | tf_op jit(solution)/shard_map/all_to_all | solution.py:152
